TPU v7x, 32 devices: a whole 2x2x4 slice. The times are simulated.
32 devices in a mesh: dp: 8 (over y, x, core), mp: 4 (over z).
Axes of the slice: x: 2, y: 2, z: 4, core: 2. Of those that a mesh axis runs over, the one named last changes fastest.
Arguments:
- factor_rows: bfloat16 [4, 8, 8, 768], P('mp', None, 'dp')
- old_statistic: float32 [8, 4, 768, 768], P('dp', 'mp'), may hold values from -1 to 2, as said below
- assignment: int32 [4, 8], P('mp'), may hold values from 0 to 7, each once within a row
- gradient: bfloat16 [8, 4, 768, 512], P('dp', None, None, 'mp'), may hold values from -3 to 3
Outputs:
- update: bfloat16 [8, 4, 768, 512], P('dp', None, None, 'mp')
Inputs may be any that keep to these rules, and one draw needn't show every extreme that they name: Each row of assignment names every block number once. `old_statistic`: each block is symmetric positive definite.
All inputs are finite; a program needn't handle non-finite values.
Results may differ from a plain program's by a relative error of at most 0.001.
The roundings to bfloat16 on the way count: a program that leaves them out, or rounds other values in their place, can miss the bound.
Values may be sent and summed in bfloat16 or wider, within the bound.
No kernel may reach another device: no remote copies, remote signals or barrier semaphores. Data moves between devices by JAX's collectives and lax.ppermute only.
A program may use at most 64 MiB of HBM per device.

v0:
```python
import jax
import jax.numpy as jnp
from jax import lax
from jax.sharding import PartitionSpec as P


def newton_factors(statistic):
    identity = jnp.eye(statistic.shape[0], dtype=jnp.float32)
    frob_norm = jnp.sqrt(jnp.sum(statistic * statistic) + 1e-06)
    normed = statistic / frob_norm
    step_one = ((5.0 * identity - normed) * 0.25).astype(jnp.bfloat16)
    square_one = jnp.dot(step_one, step_one, preferred_element_type=jnp.float32).astype(
        jnp.bfloat16
    )
    product_one = jnp.dot(
        square_one, normed.astype(jnp.bfloat16), preferred_element_type=jnp.float32
    ).astype(jnp.bfloat16)
    coupled_one = jnp.dot(square_one, product_one, preferred_element_type=jnp.float32)
    step_two = ((5.0 * identity - coupled_one) * 0.25).astype(jnp.bfloat16)
    square_two = jnp.dot(step_two, step_two, preferred_element_type=jnp.float32).astype(
        jnp.bfloat16
    )
    product_two = jnp.dot(
        square_two, coupled_one.astype(jnp.bfloat16), preferred_element_type=jnp.float32
    ).astype(jnp.bfloat16)
    coupled_two = jnp.dot(square_two, product_two, preferred_element_type=jnp.float32)
    step_three = ((5.0 * identity - coupled_two) / (4.0 * jnp.sqrt(jnp.sqrt(frob_norm)))).astype(
        jnp.bfloat16
    )
    return jnp.stack([step_one, step_two, step_three])


def body(factor_rows, old_statistic, assignment, gradient):
    chosen = assignment[0]
    picked = jnp.take(factor_rows[0], chosen, axis=0)
    arrived = lax.all_to_all(picked, "dp", split_axis=0, concat_axis=1, tiled=True)
    factors = arrived[0]
    count = factors.shape[0]
    gram = lax.dot_general(
        factors, factors, (((0,), (0,)), ((), ())), preferred_element_type=jnp.float32
    )
    statistic = old_statistic[0, 0] + gram / count
    stacked = newton_factors(statistic)
    first_pass = jnp.einsum(
        "ij,nkjc->nkic",
        stacked[2],
        lax.all_to_all(gradient, "mp", split_axis=1, concat_axis=3, tiled=True),
        preferred_element_type=jnp.float32,
    ).astype(jnp.bfloat16)
    second_pass = jnp.einsum(
        "ij,nkjc->nkic", stacked[1], first_pass, preferred_element_type=jnp.float32
    ).astype(jnp.bfloat16)
    result = jnp.einsum(
        "ij,nkjc->nkic", stacked[0], second_pass, preferred_element_type=jnp.float32
    ).astype(jnp.bfloat16)
    return lax.all_to_all(result, "mp", split_axis=3, concat_axis=1, tiled=True)


def solution(mesh):
    return jax.shard_map(
        body,
        mesh=mesh,
        in_specs=(
            P("mp", None, "dp", None),
            P("dp", "mp", None, None),
            P("mp", None),
            P("dp", None, None, "mp"),
        ),
        out_specs=P("dp", None, None, "mp"),
        check_vma=False,
    )
```

profile of v0, /device:TPU:0, one launch (start us, length us, event | category | flops | bytes accessed | tf_op | source)
XLA Modules:
  0.0 77.3 jit_solution(11541387428655440850)
XLA Ops:
  0.0 0.0 copy-start
  0.0 0.7 fusion.18
  0.7 0.7 compare_and_fusion
  1.3 0.0 copy-done
  1.4 0.6 gather_fusion
  1.9 0.1 bitcast_select_fusion
  2.0 0.5 broadcast.94
  2.5 0.6 reduce
  3.2 0.6 reshape.92
  3.8 5.2 %all-to-all-start = ((bf16[8,2,384]{2,1,0:T(2,128)(2,1)}), bf16[8,2,384]{2,1,0:T(2,128)(2,1)S(1)}, u32[]{:S(2)}, u32[]{:S(2)}) async-start(bf16[8,2,384]{2,1,0:T(2,128)(2,1)} %reshape.92), calls=%async_computation | async-start | bytes 24576 | tf_op jit(solution)/shard_map/all_to_all | solution.py:36
  9.0 2.3 %copy.13 = bf16[1,4,768,128]{2,3,0,1:T(8,128)(2,1)} copy(bf16[1,4,768,128]{3,2,1,0:T(8,128)(2,1)} %param.7) | data formatting | bytes 1572864 | tf_op args[3]
  11.3 2.4 %all-to-all-done = bf16[8,2,384]{2,1,0:T(2,128)(2,1)S(1)} async-done(((bf16[8,2,384]{2,1,0:T(2,128)(2,1)}), bf16[8,2,384]{2,1,0:T(2,128)(2,1)S(1)}, u32[]{:S(2)}, u32[]{:S(2)}) %all-to-all-start) | async-done | bytes 12320 | tf_op jit(solution)/shard_map/all_to_all | solution.py:36
  13.7 4.9 %all-to-all-start.1 = ((bf16[1,4,768,128]{2,3,0,1:T(8,128)(2,1)}), bf16[1,4,768,128]{2,3,0,1:T(8,128)(2,1)}, u32[]{:S(2)}, u32[]{:S(2)}) async-start(bf16[1,4,768,128]{2,3,0,1:T(8,128)(2,1)} %copy.13), calls=%async_computation.1 | async-start | bytes 1572864 | tf_op jit(solution)/shard_map/all_to_all | solution.py:47
  18.6 3.2 %multiply_reduce_fusion = (f32[]{:T(128)}, f32[768,768]{1,0:T(8,128)S(1)}) fusion(bf16[8,1,768]{2,1,0:T(2,128)(2,1)S(1)} %reshape.93, f32[1,1,768,768]{3,2,1,0:T(8,128)} %param.5), kind=kOutput, calls=%fused_computation.11 | convolution fusion | flops 11796479 | bytes 4730884 | tf_op jit(solution)/shard_map/dot_general | solution.py:39
  22.5 0.3 fusion.1
  22.9 2.1 %convolution_convert_fusion.3 = bf16[768,768]{1,0:T(8,128)(2,1)} fusion(bf16[768,768]{1,0:T(8,128)(2,1)S(1)} %fusion.1), kind=kOutput, calls=%fused_computation.16 | convolution fusion | flops 906559488 | bytes 2359296 | tf_op jit(solution)/shard_map/dot_general | solution.py:12
  25.0 5.1 %fusion.11 = f32[768,768]{1,0:T(8,128)} fusion(bf16[768,768]{1,0:T(8,128)(2,1)} %convolution_convert_fusion.3, f32[768,768]{1,0:T(8,128)S(1)} %get-tuple-element.6, f32[]{:T(128)S(6)} %sqrt.9), kind=kOutput, calls=%fused_computation.25 | convolution fusion | flops 1813708800 | bytes 5898244 | tf_op jit(solution)/shard_map/dot_general | solution.py:18
  30.1 0.0 copy-start.1
  30.1 3.6 %convolution_convert_fusion.1 = bf16[768,768]{1,0:T(8,128)(2,1)S(1)} fusion(f32[768,768]{1,0:T(8,128)} %fusion.11), kind=kOutput, calls=%fused_computation.14 | convolution fusion | flops 909508608 | bytes 3538944 | tf_op jit(solution)/shard_map/dot_general | solution.py:20
  33.7 0.0 copy-done.1
  33.8 1.1 %convolution_convert_fusion = bf16[768,768]{1,0:T(8,128)(2,1)S(1)} fusion(bf16[768,768]{1,0:T(8,128)(2,1)S(1)} %convolution_convert_fusion.1, f32[768,768]{1,0:T(8,128)S(1)} %copy-done.1), kind=kOutput, calls=%fused_computation.13 | convolution fusion | flops 907149312 | bytes 4718592 | tf_op jit(solution)/shard_map/dot_general | solution.py:23
  34.9 3.9 %all-to-all-done.1 = bf16[1,4,768,128]{2,3,0,1:T(8,128)(2,1)} async-done(((bf16[1,4,768,128]{2,3,0,1:T(8,128)(2,1)}), bf16[1,4,768,128]{2,3,0,1:T(8,128)(2,1)}, u32[]{:S(2)}, u32[]{:S(2)}) %all-to-all-start.1) | async-done | bytes 786464 | tf_op jit(solution)/shard_map/all_to_all | solution.py:47
  38.7 3.7 %convolution_convert_fusion.6 = bf16[768,512]{1,0:T(8,128)(2,1)} fusion(bf16[768,512]{0,1:T(8,128)(2,1)} %bitcast.8, bf16[768,768]{1,0:T(8,128)(2,1)S(1)} %convolution_convert_fusion.1, bf16[768,768]{1,0:T(8,128)(2,1)S(1)} %convolution_convert_fusion, f32[]{:T(128)S(6)} %mul_shard_map.3), kind=kOutput, calls=%fused_computation.19 | convolution fusion | flops 1513291776 | bytes 3932164 | tf_op jit(solution)/shard_map/ij,nkjc->nkic/dot_general | solution.py:44
  42.5 3.5 %fusion.7 = bf16[1,1,768,512]{2,3,1,0:T(8,128)(2,1)S(1)} fusion(bf16[768,768]{1,0:T(8,128)(2,1)S(1)} %fusion.1, bf16[768,512]{1,0:T(8,128)(2,1)} %convolution_convert_fusion.6, f32[768,768]{1,0:T(8,128)} %fusion.11), kind=kOutput, calls=%fused_computation.21 | convolution fusion | flops 1211695104 | bytes 5111808 | tf_op jit(solution)/shard_map/ij,nkjc->nkic/dot_general | solution.py:53
  45.9 1.2 %copy.25 = bf16[1,1,768,512]{2,1,0,3:T(2,128)(2,1)S(1)} copy(bf16[1,1,768,512]{2,3,1,0:T(8,128)(2,1)S(1)} %fusion.7) | data formatting | bytes 1572864 | tf_op jit(solution)/shard_map/convert_element_type | solution.py:55
  47.1 5.8 %reduce.1 = bf16[512,768]{1,0:T(8,128)(2,1)S(1)} reduce(bf16[512,1,1,768]{3,2,1,0:T(2,128)(2,1)S(1)} %bitcast.60, bf16[]{:T(256)} %broadcast.94), dimensions={1,2}, to_apply=%bitcast.58.reduce_sub_computation | reduce | bytes 1572866
  52.9 0.2 reshape.94
  53.1 22.1 %all_to_all.42 = bf16[4,2,49152]{2,1,0:T(2,128)(2,1)S(1)} all-to-all(bf16[4,2,49152]{2,1,0:T(2,128)(2,1)S(1)} %reshape.94), channel_id=1, replica_groups=mesh['dp'=8,'mp'=4] {'mp'}, dimensions={0} | all-to-all | bytes 1572864 | tf_op jit(solution)/shard_map/all_to_all | solution.py:56
  75.2 0.7 reshape.95
  76.0 0.1 copy.17
  76.1 1.2 %copy.15 = bf16[1,4,768,128]{3,2,1,0:T(8,128)(2,1)} copy(bf16[1,4,768,128]{2,3,1,0:T(8,128)(2,1)S(1)} %bitcast.62) | data formatting | bytes 1572864 | tf_op jit(solution)/shard_map/all_to_all | solution.py:56
  (2 shorter events, 0.0 us)
Async XLA Ops:
  0.0 1.3 %copy-start = (bf16[1,8,1,768]{3,1,2,0:T(8,128)(2,1)S(1)}, bf16[1,8,1,768]{3,1,2,0:T(8,128)(2,1)}, u32[]{:S(2)}) copy-start(bf16[1,8,1,768]{3,1,2,0:T(8,128)(2,1)} %param.4) | copy-start | bytes 36868
  3.8 9.9 %all-to-all-start = ((bf16[8,2,384]{2,1,0:T(2,128)(2,1)}), bf16[8,2,384]{2,1,0:T(2,128)(2,1)S(1)}, u32[]{:S(2)}, u32[]{:S(2)}) async-start(bf16[8,2,384]{2,1,0:T(2,128)(2,1)} %reshape.92), calls=%async_computation | async-start | bytes 24576 | tf_op jit(solution)/shard_map/all_to_all | solution.py:36
  13.7 25.0 %all-to-all-start.1 = ((bf16[1,4,768,128]{2,3,0,1:T(8,128)(2,1)}), bf16[1,4,768,128]{2,3,0,1:T(8,128)(2,1)}, u32[]{:S(2)}, u32[]{:S(2)}) async-start(bf16[1,4,768,128]{2,3,0,1:T(8,128)(2,1)} %copy.13), calls=%async_computation.1 | async-start | bytes 1572864 | tf_op jit(solution)/shard_map/all_to_all | solution.py:47
  30.1 3.7 %copy-start.1 = (f32[768,768]{1,0:T(8,128)S(1)}, f32[768,768]{1,0:T(8,128)}, u32[]{:S(2)}) copy-start(f32[768,768]{1,0:T(8,128)} %fusion.11) | copy-start | bytes 7077892
where the time goes:
time: 77.8 us; the launch traced here: 77.3 us
  matrix products  22.3 us (29%)
  blocking collectives  22.1 us (28%)
  starting transfers between devices  10.1 us (13%)
  other arithmetic  8.12 us (10%)
  local copies, waits for them, and re-layouts  7.49 us (10%)
  waiting for transfers between devices  6.3 us (8%)
  between operations  0.93 us (1%)
    all_to_all x1, blocking collectives, body(): return lax.all_to_all(result, 'mp', split_axis=3, concat_axis=1, tiled=True)  22.1 us
    unnamed x1, other arithmetic  5.77 us
    all_to_all x1, starting transfers between devices, body(): lax.all_to_all(picked, 'dp', split_axis=0, concat_axis=1, tiled=True)  5.2 us
    dot_general x1, matrix products, newton_factors(): jnp.dot(square_one, product_one, preferred_element_type=jnp.float32)  5.06 us
    all_to_all x1, starting transfers between devices, body(): lax.all_to_all(gradient, 'mp', split_axis=1, concat_axis=3, tiled=True)  4.87 us
    unnamed x10, local copies, waits for them, and re-layouts  4 us
    all_to_all x1, waiting for transfers between devices, body(): lax.all_to_all(gradient, 'mp', split_axis=1, concat_axis=3, tiled=True)  3.85 us
    dot_general x1, matrix products, body(): jnp.einsum('ij,nkjc->nkic', stacked[2], lax.all_to_all(gradient, 'mp', sp...  3.71 us
  transfers between devices with their start and end apart: 2, of which 2 were waited for; matrix products, arithmetic and copies ran while one was open for 23% of the time, Pallas kernels for 0%

commit v1 on v0

--- a/solution.py
+++ b/solution.py
@@ -53,7 +53,10 @@
     result = jnp.einsum(
         "ij,nkjc->nkic", stacked[0], second_pass, preferred_element_type=jnp.float32
     ).astype(jnp.bfloat16)
-    return lax.all_to_all(result, "mp", split_axis=3, concat_axis=1, tiled=True)
+    return jnp.concatenate(
+        lax.all_to_all(jnp.stack(jnp.split(result, lax.axis_size("mp"), axis=3)), "mp", 0, 0),
+        axis=1,
+    )
 
 
 def solution(mesh):

time: 77.8 us -> 69.8 us (0.90)
  other arithmetic: 8.12 us -> 2.49 us
  local copies, waits for them, and re-layouts: 7.49 us -> 5.21 us
    unnamed x1 -> x0, other arithmetic: 5.77 us -> none
    convert_element_type x1 -> x0, local copies, waits for them, and re-layouts: 1.21 us -> none  [body(): result = jnp.einsum('ij,nkjc->nkic', stacked[0], second_pass, preferred_e...]
    all_to_all x1 -> x0, local copies, waits for them, and re-layouts: 1.15 us -> none  [body(): return lax.all_to_all(result, 'mp', split_axis=3, concat_axis=1, tiled=True)]
    reshape x0 -> x1, local copies, waits for them, and re-layouts: none -> 1.15 us  [body(): jnp.concatenate(lax.all_to_all(jnp.stack(jnp.split(result, lax.axis_size(...]
    unnamed x10 -> x7, local copies, waits for them, and re-layouts: 4 us -> 2.92 us
  transfers between devices with their start and end apart: 2 -> 2, of which waited for: 2 -> 2; matrix products, arithmetic and copies ran while one was open for 23% -> 26% of each run, Pallas kernels for 0% -> 0%
where the time goes in v1:
time: 69.8 us; the launch traced here: 69.3 us
  matrix products  22.2 us (32%)
  blocking collectives  22.1 us (32%)
  starting transfers between devices  10.1 us (14%)
  waiting for transfers between devices  6.38 us (9%)
  local copies, waits for them, and re-layouts  5.21 us (7%)
  other arithmetic  2.49 us (4%)
  between operations  0.85 us (1%)
    all_to_all x1, blocking collectives, body(): lax.all_to_all(jnp.stack(jnp.split(result, lax.axis_size('mp'), axis=3)),...  22.1 us
    all_to_all x1, starting transfers between devices, body(): lax.all_to_all(picked, 'dp', split_axis=0, concat_axis=1, tiled=True)  5.2 us
    dot_general x1, matrix products, newton_factors(): jnp.dot(square_one, product_one, preferred_element_type=jnp.float32)  5.06 us
    all_to_all x1, starting transfers between devices, body(): lax.all_to_all(gradient, 'mp', split_axis=1, concat_axis=3, tiled=True)  4.87 us
    all_to_all x1, waiting for transfers between devices, body(): lax.all_to_all(gradient, 'mp', split_axis=1, concat_axis=3, tiled=True)  3.94 us
    dot_general x1, matrix products, body(): jnp.einsum('ij,nkjc->nkic', stacked[2], lax.all_to_all(gradient, 'mp', sp...  3.71 us
    dot_general x1, matrix products, newton_factors(): jnp.dot(step_two, step_two, preferred_element_type=jnp.float32)  3.65 us
    dot_general x1, matrix products, body(): jnp.einsum('ij,nkjc->nkic', stacked[0], second_pass, preferred_element_ty...  3.45 us
  transfers between devices with their start and end apart: 2, of which 2 were waited for; matrix products, arithmetic and copies ran while one was open for 26% of the time, Pallas kernels for 0%

profile of v1, /device:TPU:0, one launch (start us, length us, event | category | flops | bytes accessed | tf_op | source)
XLA Modules:
  0.0 69.3 jit_solution(7458778333132570373)
XLA Ops:
  0.0 0.0 copy-start
  0.0 0.7 fusion.18
  0.7 0.7 compare_and_fusion
  1.3 0.0 copy-done
  1.4 0.6 gather_fusion
  1.9 0.1 bitcast_select_fusion
  2.0 0.5 broadcast.94
  2.5 0.6 reduce
  3.2 0.6 reshape.96
  3.8 5.2 %all-to-all-start = ((bf16[8,2,384]{2,1,0:T(2,128)(2,1)}), bf16[8,2,384]{2,1,0:T(2,128)(2,1)S(1)}, u32[]{:S(2)}, u32[]{:S(2)}) async-start(bf16[8,2,384]{2,1,0:T(2,128)(2,1)} %reshape.96), calls=%async_computation | async-start | bytes 24576 | tf_op jit(solution)/shard_map/all_to_all | solution.py:36
  9.0 2.3 %copy.12 = bf16[1,4,768,128]{2,3,0,1:T(8,128)(2,1)} copy(bf16[1,4,768,128]{3,2,1,0:T(8,128)(2,1)} %param.7) | data formatting | bytes 1572864 | tf_op args[3]
  11.3 2.4 %all-to-all-done = bf16[8,2,384]{2,1,0:T(2,128)(2,1)S(1)} async-done(((bf16[8,2,384]{2,1,0:T(2,128)(2,1)}), bf16[8,2,384]{2,1,0:T(2,128)(2,1)S(1)}, u32[]{:S(2)}, u32[]{:S(2)}) %all-to-all-start) | async-done | bytes 12320 | tf_op jit(solution)/shard_map/all_to_all | solution.py:36
  13.7 4.9 %all-to-all-start.1 = ((bf16[1,4,768,128]{2,3,0,1:T(8,128)(2,1)}), bf16[1,4,768,128]{2,3,0,1:T(8,128)(2,1)}, u32[]{:S(2)}, u32[]{:S(2)}) async-start(bf16[1,4,768,128]{2,3,0,1:T(8,128)(2,1)} %copy.12), calls=%async_computation.1 | async-start | bytes 1572864 | tf_op jit(solution)/shard_map/all_to_all | solution.py:47
  18.6 3.2 %multiply_reduce_fusion = (f32[]{:T(128)}, f32[768,768]{1,0:T(8,128)S(1)}) fusion(bf16[8,1,768]{2,1,0:T(2,128)(2,1)S(1)} %reshape.97, f32[1,1,768,768]{3,2,1,0:T(8,128)} %param.5), kind=kOutput, calls=%fused_computation.11 | convolution fusion | flops 11796479 | bytes 4730884 | tf_op jit(solution)/shard_map/dot_general | solution.py:39
  22.5 0.3 fusion.1
  22.8 2.1 %convolution_convert_fusion.3 = bf16[768,768]{1,0:T(8,128)(2,1)} fusion(bf16[768,768]{1,0:T(8,128)(2,1)S(1)} %fusion.1), kind=kOutput, calls=%fused_computation.16 | convolution fusion | flops 906559488 | bytes 2359296 | tf_op jit(solution)/shard_map/dot_general | solution.py:12
  25.0 5.1 %fusion.11 = f32[768,768]{1,0:T(8,128)} fusion(bf16[768,768]{1,0:T(8,128)(2,1)} %convolution_convert_fusion.3, f32[768,768]{1,0:T(8,128)S(1)} %get-tuple-element.10, f32[]{:T(128)S(6)} %sqrt.9), kind=kOutput, calls=%fused_computation.25 | convolution fusion | flops 1813708800 | bytes 5898244 | tf_op jit(solution)/shard_map/dot_general | solution.py:18
  30.0 0.0 copy-start.1
  30.0 3.6 %convolution_convert_fusion.1 = bf16[768,768]{1,0:T(8,128)(2,1)S(1)} fusion(f32[768,768]{1,0:T(8,128)} %fusion.11), kind=kOutput, calls=%fused_computation.14 | convolution fusion | flops 909508608 | bytes 3538944 | tf_op jit(solution)/shard_map/dot_general | solution.py:20
  33.7 0.0 copy-done.1
  33.7 1.1 %convolution_convert_fusion = bf16[768,768]{1,0:T(8,128)(2,1)S(1)} fusion(bf16[768,768]{1,0:T(8,128)(2,1)S(1)} %convolution_convert_fusion.1, f32[768,768]{1,0:T(8,128)S(1)} %copy-done.1), kind=kOutput, calls=%fused_computation.13 | convolution fusion | flops 907149312 | bytes 4718592 | tf_op jit(solution)/shard_map/dot_general | solution.py:23
  34.8 3.9 %all-to-all-done.1 = bf16[1,4,768,128]{2,3,0,1:T(8,128)(2,1)} async-done(((bf16[1,4,768,128]{2,3,0,1:T(8,128)(2,1)}), bf16[1,4,768,128]{2,3,0,1:T(8,128)(2,1)}, u32[]{:S(2)}, u32[]{:S(2)}) %all-to-all-start.1) | async-done | bytes 786464 | tf_op jit(solution)/shard_map/all_to_all | solution.py:47
  38.8 3.7 %convolution_convert_fusion.6 = bf16[768,512]{1,0:T(8,128)(2,1)} fusion(bf16[768,512]{0,1:T(8,128)(2,1)} %bitcast.8, bf16[768,768]{1,0:T(8,128)(2,1)S(1)} %convolution_convert_fusion.1, bf16[768,768]{1,0:T(8,128)(2,1)S(1)} %convolution_convert_fusion, f32[]{:T(128)S(6)} %mul_shard_map.3), kind=kOutput, calls=%fused_computation.19 | convolution fusion | flops 1513291776 | bytes 3932164 | tf_op jit(solution)/shard_map/ij,nkjc->nkic/dot_general | solution.py:44
  42.5 3.5 %fusion.7 = bf16[1,1,768,512]{2,3,1,0:T(8,128)(2,1)S(1)} fusion(bf16[768,768]{1,0:T(8,128)(2,1)S(1)} %fusion.1, bf16[768,512]{1,0:T(8,128)(2,1)} %convolution_convert_fusion.6, f32[768,768]{1,0:T(8,128)} %fusion.11), kind=kOutput, calls=%fused_computation.21 | convolution fusion | flops 1211695104 | bytes 5111808 | tf_op jit(solution)/shard_map/ij,nkjc->nkic/dot_general | solution.py:53
  45.9 0.1 slice_bitcast_fusion.3
  46.0 0.1 pad_maximum_fusion
  46.1 22.1 %all_to_all.29 = bf16[4,1,1,768,128]{3,4,2,1,0:T(8,128)(2,1)S(1)} all-to-all(bf16[4,1,1,768,128]{3,4,2,1,0:T(8,128)(2,1)S(1)} %pad_maximum_fusion), channel_id=1, replica_groups=mesh['dp'=8,'mp'=4] {'mp'}, dimensions={0} | all-to-all | bytes 1572864 | tf_op jit(solution)/shard_map/all_to_all | solution.py:57
  68.2 1.2 %copy.13 = bf16[1,4,768,128]{3,2,1,0:T(8,128)(2,1)} copy(bf16[1,4,768,128]{2,3,1,0:T(8,128)(2,1)S(1)} %bitcast.60) | data formatting | bytes 1572864 | tf_op jit(solution)/shard_map/reshape | solution.py:56
  (2 shorter events, 0.0 us)
Async XLA Ops:
  0.0 1.3 %copy-start = (bf16[1,8,1,768]{3,1,2,0:T(8,128)(2,1)S(1)}, bf16[1,8,1,768]{3,1,2,0:T(8,128)(2,1)}, u32[]{:S(2)}) copy-start(bf16[1,8,1,768]{3,1,2,0:T(8,128)(2,1)} %param.4) | copy-start | bytes 36868
  3.8 9.9 %all-to-all-start = ((bf16[8,2,384]{2,1,0:T(2,128)(2,1)}), bf16[8,2,384]{2,1,0:T(2,128)(2,1)S(1)}, u32[]{:S(2)}, u32[]{:S(2)}) async-start(bf16[8,2,384]{2,1,0:T(2,128)(2,1)} %reshape.96), calls=%async_computation | async-start | bytes 24576 | tf_op jit(solution)/shard_map/all_to_all | solution.py:36
  13.7 25.0 %all-to-all-start.1 = ((bf16[1,4,768,128]{2,3,0,1:T(8,128)(2,1)}), bf16[1,4,768,128]{2,3,0,1:T(8,128)(2,1)}, u32[]{:S(2)}, u32[]{:S(2)}) async-start(bf16[1,4,768,128]{2,3,0,1:T(8,128)(2,1)} %copy.12), calls=%async_computation.1 | async-start | bytes 1572864 | tf_op jit(solution)/shard_map/all_to_all | solution.py:47
  30.0 3.7 %copy-start.1 = (f32[768,768]{1,0:T(8,128)S(1)}, f32[768,768]{1,0:T(8,128)}, u32[]{:S(2)}) copy-start(f32[768,768]{1,0:T(8,128)} %fusion.11) | copy-start | bytes 7077892
